TPU v7x, 32 devices: a whole 2x2x4 slice. The times are simulated.
32 devices in a mesh: bin: 4 (over x, core), frame: 8 (over z, y).
Axes of the slice: x: 2, y: 2, z: 4, core: 2. Of those that a mesh axis runs over, the one named last changes fastest.
Arguments:
- signal: bfloat16 [32, 2, 256, 2048], P('bin', None, None, 'frame'), may hold values from -24 to 24
- demix: float32 [32, 256, 512], P('bin'), may hold values from -1 to 2
Outputs:
- demixed: float32 [32, 256, 512], P('bin', 'frame')
- gradient: float32 [32, 256, 512], P('bin', 'frame')
All inputs are finite; a program needn't handle non-finite values.
Results may differ from a plain program's by a relative error of at most 0.0061.
Values sent between devices are 32-bit elements; how exact they have to be, the bound alone decides.
A program may use at most 64 MiB of HBM per device.

v0:
```python
import jax
import jax.numpy as jnp
from jax import lax
from jax.sharding import PartitionSpec as P

BINS = 32
ITERS = 2


step_size = 0.05
small_eps = 1e-06


def complex_matrix(demixing):
    width = demixing.shape[-1] // 2
    real_part = demixing[..., :width]
    imag_part = demixing[..., width:]
    upper = jnp.concatenate([real_part, imag_part], axis=-1)
    lower = jnp.concatenate([-imag_part, real_part], axis=-1)
    return jnp.concatenate([upper, lower], axis=-2)


def on_device(signal, demix):
    frame_local = signal.shape[-1]
    group_size = lax.axis_size("frame")
    frame_total = frame_local * group_size
    source_count = demix.shape[1]
    row_total = source_count // group_size
    first_own = lax.axis_index("frame") * row_total
    real_in = signal[:, 0]
    imag_in = signal[:, 1]
    stacked = jnp.concatenate(
        [
            jnp.concatenate([real_in, imag_in], axis=-1),
            jnp.concatenate([-imag_in, real_in], axis=-1),
        ],
        axis=-2,
    )
    demixing = demix
    result = lax.dynamic_slice_in_dim(demix, first_own, row_total, 1)
    direction_out = result
    for iteration in range(ITERS):
        rounded = demixing.astype(jnp.bfloat16)
        sources = jnp.einsum("fkj,fjt->fkt", rounded, stacked, preferred_element_type=jnp.float32)
        squares = jnp.sum(sources * sources, axis=0)
        local_power = squares[:, :frame_local] + squares[:, frame_local:]
        power_sum = lax.psum(local_power, "bin")
        radius = jnp.sqrt(power_sum / BINS + small_eps)
        radius_both = jnp.concatenate([radius, radius], axis=1)
        scored = (sources / radius_both[None]).astype(jnp.bfloat16)
        source_b = sources.astype(jnp.bfloat16)
        imag_key = jnp.concatenate(
            [-source_b[:, :, frame_local:], source_b[:, :, :frame_local]], axis=2
        )
        both_keys = jnp.concatenate([source_b, imag_key], axis=1)
        partial_gram = jnp.einsum(
            "fkt,flt->kfl", scored, both_keys, preferred_element_type=jnp.float32
        )
        gram_rows = lax.psum_scatter(
            partial_gram / frame_total, "frame", scatter_dimension=0, tiled=True
        )
        gram_rows = jnp.transpose(gram_rows, (1, 0, 2))
        own_rows = lax.dynamic_slice_in_dim(demixing, first_own, row_total, 1)
        product = jnp.einsum(
            "fkj,fjl->fkl", gram_rows, complex_matrix(demixing), precision=lax.Precision.HIGHEST
        )
        own_direction = own_rows - product
        new_rows = own_rows + step_size * own_direction
        if iteration + 1 < ITERS:
            demixing = lax.all_gather(new_rows, "frame", axis=1, tiled=True)
        else:
            result = new_rows
            direction_out = own_direction
    return (result, direction_out)


def solution(mesh):
    placed = (P("bin", None, None, "frame"), P("bin", None, None))
    return jax.shard_map(
        on_device,
        mesh=mesh,
        in_specs=placed,
        out_specs=(P("bin", "frame", None), P("bin", "frame", None)),
        check_vma=False,
    )
```

profile of v0, /device:TPU:0, one launch (start us, length us, event | category | flops | bytes accessed | tf_op | source)
XLA Modules:
  0.0 391.5 jit_solution(2403866182730750756)
XLA Ops:
  7.2 1.7 fusion.60
  8.9 0.5 copy.38
  9.4 0.1 bitcast_negate_fusion
  9.5 1.4 copy.37
  10.9 6.2 %fusion.24 = (f32[256,512]{0,1:T(8,128)S(1)}, f32[8,512,256]{2,1,0:T(8,128)}) fusion(f32[8,256,512]{2,1,0:T(8,128)} %param.3, bf16[8,256,256]{1,2,0:T(8,128)(2,1)} %bitcast.22, bf16[8,256,256]{1,2,0:T(8,128)(2,1)S(1)} %bitcast_negate_fusion, bf16[8,256,256]{1,2,0:T(8,128)(2,1)S(1)} %bitcast.20), kind=kOutput, calls=%fused_computation.28 | convolution fusion | flops 1093533696 | bytes 12058624 | tf_op jit(solution)/shard_map/fkj,fjt->fkt/dot_general | solution.py:44
  17.1 0.7 slice_add_fusion
  17.9 0.0 reduce-scatter.3.cloned.1.call-start
  17.9 2.4 bitcast_convert_fusion
  20.4 1.4 slice_negate_fusion.3
  21.8 31.2 %all-reduce.3.cloned.1.call-done = f32[256,256]{0,1:T(8,128)} async-done(((f32[256,256]{0,1:T(8,128)}), f32[256,256]{0,1:T(8,128)}) %all-reduce.3.cloned.1.call-update) | async-done | bytes 262160 | tf_op jit(solution)/shard_map/psum | solution.py:47
  53.0 1.0 add_sqrt_fusion.1
  54.1 6.4 %multiply_bitcast_fusion.1 = f32[256,8,512]{0,2,1:T(8,128)} fusion(f32[8,512,256]{2,1,0:T(8,128)} %get-tuple-element.17, f32[256,512]{0,1:T(8,128)S(1)} %pad_maximum_fusion, bf16[8,256,256]{1,2,0:T(8,128)(2,1)} %get-tuple-element.11, bf16[8,256,256]{1,2,0:T(8,128)(2,1)} %get-tuple-element.10, bf16[8,256,512]{1,2,0:T(8,128)(2,1)S(1)} %bitcast_convert_fusion), kind=kOutput, calls=%fused_computation.33 | convolution fusion | flops 1089470464 | bytes 13107200 | tf_op jit(solution)/shard_map/fkt,flt->kfl/dot_general | solution.py:56
  60.5 5.6 %copy.26 = f32[256,8,512]{2,1,0:T(8,128)} copy(f32[256,8,512]{0,2,1:T(8,128)} %multiply_bitcast_fusion.1) | data formatting | bytes 8388608 | tf_op jit(solution)/shard_map/div | solution.py:60
  66.1 0.0 all-gather.2.cloned.1.call-start
  66.1 4.0 %slice_negate_fusion.1 = (f32[8,256,256]{2,1,0:T(8,128)S(1)}, f32[8,256,256]{2,1,0:T(8,128)}) fusion(f32[8,256,512]{2,1,0:T(8,128)} %param.3), kind=kLoop, calls=%fused_computation.38 | loop fusion | flops 524288 | bytes 8388608 | tf_op jit(solution)/shard_map/neg | solution.py:19
  70.1 84.4 %reduce-scatter.3.cloned.1.call-done = f32[32,8,512]{2,1,0:T(8,128)} async-done(((f32[256,8,512]{2,1,0:T(8,128)}), f32[32,8,512]{2,1,0:T(8,128)}) %reduce-scatter.3.cloned.1.call-update) | async-done | bytes 524304 | tf_op jit(solution)/shard_map/reduce_scatter | solution.py:59
  154.5 8.8 %fusion.48 = f32[8,32,512]{2,1,0:T(8,128)} fusion(f32[8,256,256]{2,1,0:T(8,128)} %get-tuple-element.7, f32[8,256,256]{2,1,0:T(8,128)S(1)} %get-tuple-element.6, f32[8,256,512]{2,1,0:T(8,128)} %param.3, f32[8,32,512]{2,0,1:T(8,128)} %bitcast.24, s32[]{:T(128)S(6)} %select_n.4), kind=kOutput, calls=%fused_computation.45 | convolution fusion | flops 809893888 | bytes 9961476 | tf_op jit(solution)/shard_map/fkj,fjl->fkl/dot_general | solution.py:64
  163.4 72.5 %all-gather.2.cloned.1.call-done = f32[8,256,512]{2,1,0:T(8,128)} async-done(((f32[8,32,512]{2,1,0:T(8,128)}), f32[8,256,512]{2,1,0:T(8,128)}) %all-gather.2.cloned.1.call-update) | async-done | bytes 4194320 | tf_op jit(solution)/shard_map/all_gather | solution.py:70
  235.9 6.5 %fusion.59 = (bf16[8,256,512]{2,1,0:T(8,128)(2,1)S(1)}, f32[256,512]{1,0:T(8,128)S(1)}, f32[8,256,512]{2,1,0:T(8,128)}) fusion(bf16[8,256,256]{1,2,0:T(8,128)(2,1)} %bitcast.23, bf16[8,256,256]{1,2,0:T(8,128)(2,1)} %copy-done, bf16[8,256,256]{1,2,0:T(8,128)(2,1)S(1)} %bitcast.21, f32[8,256,512]{2,1,0:T(8,128)} %all-gather.2.cloned.1.call-done), kind=kOutput, calls=%fused_computation.63 | convolution fusion | flops 1094582272 | bytes 14155776 | tf_op jit(solution)/shard_map/fkj,fjt->fkt/dot_general | solution.py:44
  242.5 0.1 copy.39
  242.6 0.1 copy.40
  242.8 0.7 add.34
  243.5 0.2 reduce-scatter.5.cloned.1.call-start
  243.8 1.5 slice_negate_fusion.2
  245.3 29.2 %all-reduce.5.cloned.1.call-done = f32[256,256]{0,1:T(8,128)} async-done(((f32[256,256]{0,1:T(8,128)}), f32[256,256]{0,1:T(8,128)}) %all-reduce.5.cloned.1.call-update) | async-done | bytes 262160 | tf_op jit(solution)/shard_map/psum | solution.py:47
  274.5 1.0 add_sqrt_fusion
  275.6 0.2 copy.31
  275.8 6.1 %multiply_bitcast_fusion = f32[256,8,512]{0,2,1:T(8,128)} fusion(f32[8,256,512]{2,1,0:T(8,128)} %get-tuple-element.18, f32[256,512]{1,0:T(8,128)S(1)} %copy.31, bf16[8,256,256]{2,1,0:T(8,128)(2,1)} %get-tuple-element.9, bf16[8,256,256]{2,1,0:T(8,128)(2,1)} %get-tuple-element.8, bf16[8,256,512]{2,1,0:T(8,128)(2,1)S(1)} %get-tuple-element.2), kind=kOutput, calls=%fused_computation.30 | convolution fusion | flops 1089470464 | bytes 13107200 | tf_op jit(solution)/shard_map/fkt,flt->kfl/dot_general | solution.py:56
  281.9 5.6 %copy.32 = f32[256,8,512]{2,1,0:T(8,128)} copy(f32[256,8,512]{0,2,1:T(8,128)} %multiply_bitcast_fusion) | data formatting | bytes 8388608 | tf_op jit(solution)/shard_map/div | solution.py:60
  287.5 4.0 %slice_negate_fusion = (f32[8,256,256]{2,1,0:T(8,128)S(1)}, f32[8,256,256]{2,1,0:T(8,128)}) fusion(f32[8,256,512]{2,1,0:T(8,128)} %all-gather.2.cloned.1.call-done), kind=kLoop, calls=%fused_computation.34 | loop fusion | flops 524288 | bytes 8388608 | tf_op jit(solution)/shard_map/neg | solution.py:19
  291.5 84.5 %reduce-scatter.5.cloned.1.call-done = f32[32,8,512]{2,1,0:T(8,128)} async-done(((f32[256,8,512]{2,1,0:T(8,128)}), f32[32,8,512]{2,1,0:T(8,128)}) %reduce-scatter.5.cloned.1.call-update) | async-done | bytes 524304 | tf_op jit(solution)/shard_map/reduce_scatter | solution.py:59
  376.0 9.0 %multiply_add_fusion = (f32[8,32,512]{2,1,0:T(8,128)}, f32[8,32,512]{2,1,0:T(8,128)}) fusion(f32[8,256,512]{2,1,0:T(8,128)} %all-gather.2.cloned.1.call-done, s32[]{:T(128)S(6)} %select_n.4, f32[8,256,256]{2,1,0:T(8,128)} %get-tuple-element.5, f32[8,256,256]{2,1,0:T(8,128)S(1)} %get-tuple-element.4, f32[8,32,512]{2,0,1:T(8,128)} %bitcast.25), kind=kOutput, calls=%fused_computation.52 | convolution fusion | flops 809893888 | bytes 10485764 | tf_op jit(solution)/shard_map/fkj,fjl->fkl/dot_general | solution.py:64
  (12 shorter events, 0.3 us)
Async XLA Ops:
  7.2 45.9 %all-reduce.3.cloned.1.call-start = ((), (), s32[]{:S(2)}) async-start(), calls=%async_computation.2 | async-start | bytes 524288 | tf_op jit(solution)/shard_map/psum | solution.py:47
  9.5 7.6 %copy-start = (bf16[8,256,256]{1,2,0:T(8,128)(2,1)}, bf16[8,256,256]{1,2,0:T(8,128)(2,1)S(1)}, u32[]{:S(2)}) copy-start(bf16[8,256,256]{1,2,0:T(8,128)(2,1)S(1)} %bitcast_negate_fusion) | copy-start | bytes 3145732
  17.9 136.6 %reduce-scatter.3.cloned.1.call-start = ((), (), s32[]{:S(2)}) async-start(), calls=%async_computation.3 | async-start | bytes 4718592 | tf_op jit(solution)/shard_map/reduce_scatter | solution.py:59
  66.1 169.9 %all-gather.2.cloned.1.call-start = ((), (), s32[]{:S(2)}) async-start(), calls=%async_computation.4 | async-start | bytes 4718592 | tf_op jit(solution)/shard_map/all_gather | solution.py:70
  163.3 111.2 %all-reduce.5.cloned.1.call-start = ((), (), s32[]{:S(2)}) async-start(), calls=%async_computation.5 | async-start | bytes 524288 | tf_op jit(solution)/shard_map/psum | solution.py:47
  243.5 132.4 %reduce-scatter.5.cloned.1.call-start = ((), (), s32[]{:S(2)}) async-start(), calls=%async_computation.6 | async-start | bytes 4718592 | tf_op jit(solution)/shard_map/reduce_scatter | solution.py:59
Sparse Core Ops, SparseCore 0:
  18.0 34.9 all-reduce.2
  66.2 88.2 reduce-scatter.2
  163.5 72.4 all-gather.1
  243.7 30.8 all-reduce.4
  287.6 88.2 reduce-scatter.4
where the time goes:
time: 392 us; the launch traced here: 391 us
  waiting for transfers between devices  302 us (77%)
  matrix products  43 us (11%)
  other arithmetic  17 us (4%)
  local copies, waits for them, and re-layouts  15.2 us (4%)
  between operations  13.9 us (4%)
    reduce_scatter x2, waiting for transfers between devices, on_device(): lax.psum_scatter(partial_gram / frame_total, 'frame', scatter_dimension=0...  169 us
    all_gather x1, waiting for transfers between devices, on_device(): demixing = lax.all_gather(new_rows, 'frame', axis=1, tiled=True)  72.5 us
    psum x2, waiting for transfers between devices, on_device(): power_sum = lax.psum(local_power, 'bin')  60.5 us
    dot_general x2, matrix products, on_device(): jnp.einsum('fkj,fjl->fkl', gram_rows, complex_matrix(demixing), precision...  17.8 us
    dot_general x2, matrix products, on_device(): jnp.einsum('fkj,fjt->fkt', rounded, stacked, preferred_element_type=jnp.f...  12.8 us
    dot_general x2, matrix products, on_device(): jnp.einsum('fkt,flt->kfl', scored, both_keys, preferred_element_type=jnp....  12.5 us
    div x2, local copies, waits for them, and re-layouts, on_device(): partial_gram / frame_total  11.2 us
    neg x2, other arithmetic, complex_matrix(): lower = jnp.concatenate([-imag_part, real_part], axis=-1)  7.96 us
  transfers between devices with their start and end apart: 5, of which 5 were waited for; matrix products, arithmetic and copies ran while one was open for 3% of the time, Pallas kernels for 0%

commit v1 on v0

v1 whole, which is shorter than its diff:
```python
import functools

import jax
import jax.numpy as jnp
from jax import lax
from jax.experimental import pallas as pl
from jax.experimental.pallas import tpu as pltpu
from jax.sharding import PartitionSpec as P

ITERS = 2

step_size = 0.05
small_eps = 1e-06

MESH = pl.DeviceIdType.MESH
NT = (((1,), (1,)), ((), ()))


def dot(a, b):
    return jnp.dot(a, b, preferred_element_type=jnp.float32)


def dot_nt(a, b):
    return lax.dot_general(a, b, NT, preferred_element_type=jnp.float32)


def kernel(
    group, bin_group, sig, w_in, w_out, d_out,
    flat, w_next, src, gram, ry, part, rz, power, pw_recv, pw_sum, rinv,
    pw_send_sem, pw_recv_sem, y_send, y_recv, z_send, z_recv, ga_send, ga_recv, gy_send, gy_recv,
):
    nb, outer, _, rows, width2 = w_in.shape
    width = width2 // 2
    nt = sig.shape[3]
    total = 2 * outer * rows
    half = total // 2
    frames = nt * group
    bins = nb * bin_group
    me = lax.axis_index("frame")
    mb = lax.axis_index("bin")
    y = lax.rem(me, 2)
    yo = 1 - y
    z = me // 2
    core = lax.rem(mb, 2)
    core_o = 1 - core
    y_dev = {"frame": z * 2 + yo}
    core_dev = {"bin": mb + 1 - 2 * core}
    x_dev = {"bin": lax.rem(mb + 2, bin_group)}
    peers = [{"frame": lax.rem(z + k, outer) * 2 + y} for k in range(1, outer)]

    barrier = pltpu.get_barrier_semaphore()
    for dev in [y_dev, core_dev, x_dev] + peers:
        pl.semaphore_signal(barrier, inc=1, device_id=dev, device_id_type=MESH)
    pl.semaphore_wait(barrier, 3 + len(peers))

    def remote(a, b, s, r, dev):
        return pltpu.make_async_remote_copy(
            src_ref=a, dst_ref=b, send_sem=s, recv_sem=r, device_id=dev, device_id_type=MESH
        )

    def y_copy(it, f):
        return remote(gram.at[it, f, yo], ry.at[it, f], y_send.at[it, f], y_recv.at[it, f], y_dev)

    def z_copy(it, f, k):
        return remote(
            part.at[it, f, lax.rem(z + k, outer)], rz.at[it, f, k - 1],
            z_send.at[it, f], z_recv.at[it, f], peers[k - 1],
        )

    def many(ref, sem):
        return pltpu.make_async_copy(ref, ref, sem)

    def ga_copy(f, k):
        own = w_next.at[f, y, z]
        return remote(own, own, ga_send.at[f], ga_recv.at[f], peers[k - 1])

    def gy_copy(f):
        ref = w_next.at[f, y]
        return remote(ref, ref, gy_send.at[f], gy_recv.at[f], y_dev)

    for it in range(ITERS):
        power[...] = jnp.zeros_like(power)

        def make_sources(f, carry):
            if it > 0:
                other = w_next.at[f, yo]
                remote(other, other, gy_send.at[f], gy_recv.at[f], y_dev).wait_recv()
            for d in range(group):
                if it == 0:
                    block = w_in[f, d // 2, d % 2]
                else:
                    block = w_next[f, d % 2, d // 2]
                flat[f, d * rows:(d + 1) * rows, :] = block
            wr = flat[f, :, :width].astype(jnp.bfloat16)
            wi = flat[f, :, width:].astype(jnp.bfloat16)
            xr = sig[f, 0]
            xi = sig[f, 1]
            yr = dot(wr, xr) - dot(wi, xi)
            yi = dot(wr, xi) + dot(wi, xr)
            src[f, 0] = yr
            src[f, 1] = yi
            power[...] += yr * yr + yi * yi
            return carry

        lax.fori_loop(0, nb, make_sources, 0)

        own_half = pl.ds(pl.multiple_of(core * half, half), half)
        other_half = pl.ds(pl.multiple_of(core_o * half, half), half)
        first = remote(
            power.at[other_half], pw_recv.at[it, 0], pw_send_sem.at[it, 0], pw_recv_sem.at[it, 0], core_dev
        )
        first.start()
        first.wait()
        pw_sum[it, 0] = power[own_half, :] + pw_recv[it, 0]
        second = remote(
            pw_sum.at[it, 0], pw_recv.at[it, 1], pw_send_sem.at[it, 1], pw_recv_sem.at[it, 1], x_dev
        )
        second.start()
        second.wait()
        pw_sum[it, 1] = pw_sum[it, 0] + pw_recv[it, 1]
        third = remote(
            pw_sum.at[it, 1], pw_recv.at[it, 2], pw_send_sem.at[it, 2], pw_recv_sem.at[it, 2], core_dev
        )
        third.start()
        rinv[own_half, :] = 1.0 / jnp.sqrt(pw_sum[it, 1] / bins + small_eps)
        third.wait()
        rinv[other_half, :] = 1.0 / jnp.sqrt(pw_recv[it, 2] / bins + small_eps)

        def make_gram(f, carry):
            inv = rinv[...]
            yr = src[f, 0]
            yi = src[f, 1]
            pr = (yr * inv).astype(jnp.bfloat16)
            pi = (yi * inv).astype(jnp.bfloat16)
            br = yr.astype(jnp.bfloat16)
            bi = yi.astype(jnp.bfloat16)
            real = dot_nt(pr, br) + dot_nt(pi, bi)
            imag = dot_nt(pi, br) - dot_nt(pr, bi)
            for d in range(group):
                gram[it, f, d % 2, d // 2, :, :width] = real[d * rows:(d + 1) * rows]
                gram[it, f, d % 2, d // 2, :, width:] = imag[d * rows:(d + 1) * rows]
            y_copy(it, f).start()
            return carry

        lax.fori_loop(0, nb, make_gram, 0)

        def pair_sum(f):
            y_copy(it, f).wait_recv()
            part[it, f] = gram[it, f, y] + ry[it, f]
            for k in range(1, outer):
                z_copy(it, f, k).start()

        def update(f):
            many(rz.at[it, f], z_recv.at[it, f]).wait()
            acc = part[it, f, z]
            for k in range(outer - 1):
                acc = acc + rz[it, f, k]
            acc = acc * (1.0 / frames)
            w = flat[f]
            a = jnp.dot(acc[:, :width], w, precision=lax.Precision.HIGHEST, preferred_element_type=jnp.float32)
            b = jnp.dot(acc[:, width:], w, precision=lax.Precision.HIGHEST, preferred_element_type=jnp.float32)
            own = w_in[f, z, y] if it == 0 else w_next[f, y, z]
            dr = own[:, :width] - (a[:, :width] - b[:, width:])
            di = own[:, width:] - (a[:, width:] + b[:, :width])
            nr = own[:, :width] + step_size * dr
            ni = own[:, width:] + step_size * di
            if it + 1 < ITERS:
                w_next[f, y, z, :, :width] = nr
                w_next[f, y, z, :, width:] = ni
                for k in range(1, outer):
                    ga_copy(f, k).start()
            else:
                w_out[f, :, :width] = nr
                w_out[f, :, width:] = ni
                d_out[f, :, :width] = dr
                d_out[f, :, width:] = di

        def forward(f):
            others = w_next.at[f, y, pl.ds(0, outer - 1)]
            many(others, ga_recv.at[f]).wait()
            gy_copy(f).start()

        lag_u, lag_f = 2, 4
        last = lag_f if it + 1 < ITERS else lag_u

        def pipeline(s, carry):
            pl.when(s < nb)(lambda: pair_sum(s))
            pl.when(jnp.logical_and(s >= lag_u, s < nb + lag_u))(lambda: update(s - lag_u))
            if it + 1 < ITERS:
                pl.when(s >= lag_f)(lambda: forward(s - lag_f))
            return carry

        lax.fori_loop(0, nb + last, pipeline, 0)

    def drain(f, carry):
        for it in range(ITERS):
            y_copy(it, f).wait_send()
            many(rz.at[it, f], z_send.at[it, f]).wait()
        many(w_next.at[f, y, pl.ds(0, outer - 1)], ga_send.at[f]).wait()
        gy_copy(f).wait_send()
        return carry

    lax.fori_loop(0, nb, drain, 0)


def on_device(signal, demix):
    group = lax.axis_size("frame")
    bin_group = lax.axis_size("bin")
    nb, _, sensors, nt = signal.shape
    total, width2 = demix.shape[1:]
    rows = total // group
    outer = group // 2
    half = total // 2
    f32 = jnp.float32
    out = jax.ShapeDtypeStruct((nb, rows, width2), f32)
    dma = pltpu.SemaphoreType.DMA
    vmem = pl.BlockSpec(memory_space=pltpu.VMEM)
    return pl.pallas_call(
        functools.partial(kernel, group, bin_group),
        out_shape=(out, out),
        in_specs=[vmem, vmem],
        out_specs=(vmem, vmem),
        scratch_shapes=[
            pltpu.VMEM((nb, total, width2), f32),
            pltpu.VMEM((nb, 2, outer, rows, width2), f32),
            pltpu.VMEM((nb, 2, total, nt), f32),
            pltpu.VMEM((ITERS, nb, 2, outer, rows, width2), f32),
            pltpu.VMEM((ITERS, nb, outer, rows, width2), f32),
            pltpu.VMEM((ITERS, nb, outer, rows, width2), f32),
            pltpu.VMEM((ITERS, nb, outer - 1, rows, width2), f32),
            pltpu.VMEM((total, nt), f32),
            pltpu.VMEM((ITERS, 3, half, nt), f32),
            pltpu.VMEM((ITERS, 2, half, nt), f32),
            pltpu.VMEM((total, nt), f32),
            dma((ITERS, 3)),
            dma((ITERS, 3)),
            dma((ITERS, nb)),
            dma((ITERS, nb)),
            dma((ITERS, nb)),
            dma((ITERS, nb)),
            dma((nb,)),
            dma((nb,)),
            dma((nb,)),
            dma((nb,)),
        ],
        compiler_params=pltpu.CompilerParams(
            collective_id=0, has_side_effects=True, vmem_limit_bytes=62 * 1024 * 1024
        ),
    )(signal, demix.reshape(nb, outer, 2, rows, width2))


def solution(mesh):
    placed = (P("bin", None, None, "frame"), P("bin", None, None))
    return jax.shard_map(
        on_device,
        mesh=mesh,
        in_specs=placed,
        out_specs=(P("bin", "frame", None), P("bin", "frame", None)),
        check_vma=False,
    )
```

time: 392 us -> 197 us (0.50)
  waiting for transfers between devices: 302 us -> 0 us
  Pallas kernels: 0 us -> 192 us
  matrix products: 43 us -> 0 us
  other arithmetic: 17 us -> 0 us
  between operations: 13.9 us -> 0.64 us
  local copies, waits for them, and re-layouts: 15.2 us -> 3.74 us
    pallas_call x0 -> x1, Pallas kernels: none -> 192 us  [on_device(): pl.pallas_call(functools.partial(kernel, group, bin_group), out_shape=(ou...]
    reduce_scatter x2 -> x0, waiting for transfers between devices: 169 us -> none  [on_device(): lax.psum_scatter(partial_gram / frame_total, 'frame', scatter_dimension=0...]
    all_gather x1 -> x0, waiting for transfers between devices: 72.5 us -> none  [on_device(): demixing = lax.all_gather(new_rows, 'frame', axis=1, tiled=True)]
    psum x2 -> x0, waiting for transfers between devices: 60.5 us -> none  [on_device(): power_sum = lax.psum(local_power, 'bin')]
    dot_general x6 -> x0, matrix products: 43 us -> none  [the longest x2 17.8 us: on_device(): jnp.einsum('fkj,fjl->fkl', gram_rows, complex_matrix(demixing), precision...]
    div x2 -> x0, local copies, waits for them, and re-layouts: 11.2 us -> none  [on_device(): partial_gram / frame_total]
    neg x5 -> x0, other arithmetic: 11 us -> none  [the longest x2 7.96 us: complex_matrix(): lower = jnp.concatenate([-imag_part, real_part], axis=-1)]
  transfers between devices with their start and end apart: 5 -> 0, of which waited for: 5 -> 0; matrix products, arithmetic and copies ran while one was open for 3% -> 0% of each run, Pallas kernels for 0% -> 0%
where the time goes in v1:
time: 197 us; the launch traced here: 196 us
  Pallas kernels  192 us (97%)
  local copies, waits for them, and re-layouts  3.74 us (2%)
    pallas_call x1, Pallas kernels, on_device(): pl.pallas_call(functools.partial(kernel, group, bin_group), out_shape=(ou...  192 us

profile of v1, /device:TPU:0, one launch (start us, length us, event | category | flops | bytes accessed | tf_op | source)
XLA Modules:
  0.0 196.4 jit_solution(9509420363746035217)
XLA Ops:
  0.6 192.0 %shard_map.41 = (f32[8,32,512]{2,1,0:T(8,128)}, f32[8,32,512]{2,1,0:T(8,128)}) custom-call(bf16[8,2,256,256]{3,2,1,0:T(8,128)(2,1)} %sig.1, f32[8,4,2,32,512]{4,3,2,1,0:T(8,128)} %bitcast.1), custom_call_target="tpu_custom_call" | custom-call | tf_op jit(solution)/shard_map/pallas_call | solution.py:218
  192.6 1.9 copy.6
  194.5 1.9 copy.7

commit v2 on v1

v2 whole, which is shorter than its diff:
```python
import functools

import jax
import jax.numpy as jnp
from jax import lax
from jax.experimental import pallas as pl
from jax.experimental.pallas import tpu as pltpu
from jax.sharding import PartitionSpec as P

ITERS = 2
LAGS = (1, 2, 3, 4)

step_size = 0.05
small_eps = 1e-06

MESH = pl.DeviceIdType.MESH
NT = (((1,), (1,)), ((), ()))


def dot(a, b):
    return jnp.dot(a, b, preferred_element_type=jnp.float32)


def dot_nt(a, b):
    return lax.dot_general(a, b, NT, preferred_element_type=jnp.float32)


def kernel(
    group, bin_group, sig, w_in, w_out, d_out,
    flat, w_next, src, gram, r1, part1, r2, part2, r3, power, pw_recv, pw_sum, rinv,
    pw_send_sem, pw_recv_sem, s1_send, s1_recv, s2_send, s2_recv, s3_send, s3_recv,
    g1_send, g1_recv, g2_send, g2_recv, g3_send, g3_recv,
):
    nb, high, _, _, rows, width2 = w_in.shape
    width = width2 // 2
    nt = sig.shape[3]
    total = 4 * high * rows
    half = total // 2
    quarter = total // 4
    frames = nt * group
    bins = nb * bin_group
    me = lax.axis_index("frame")
    mb = lax.axis_index("bin")
    y = lax.rem(me, 2)
    lo = lax.rem(me // 2, 2)
    hi = me // 4
    y_step = 1 - 2 * y
    lo_step = 2 - 4 * lo
    core = lax.rem(mb, 2)
    core_o = 1 - core
    core_dev = {"bin": mb + 1 - 2 * core}
    x_dev = {"bin": lax.rem(mb + 2, bin_group)}
    peers = [{"frame": lax.rem(hi + k, high) * 4 + lax.rem(me, 4)} for k in range(1, high)]

    barrier = pltpu.get_barrier_semaphore()
    for dev in [{"frame": me + y_step}, {"frame": me + lo_step}, core_dev, x_dev] + peers:
        pl.semaphore_signal(barrier, inc=1, device_id=dev, device_id_type=MESH)
    pl.semaphore_wait(barrier, 4 + len(peers))

    def swapped(f):
        return f // (nb - nb // 8)

    def near(f):
        return y + swapped(f) * (lo - y)

    def far(f):
        return lo + swapped(f) * (y - lo)

    def near_dev(f):
        return {"frame": me + y_step + swapped(f) * (lo_step - y_step)}

    def far_dev(f):
        return {"frame": me + lo_step + swapped(f) * (y_step - lo_step)}

    def remote(a, b, s, r, dev):
        return pltpu.make_async_remote_copy(
            src_ref=a, dst_ref=b, send_sem=s, recv_sem=r, device_id=dev, device_id_type=MESH
        )

    def s1_copy(it, f):
        return remote(gram.at[it, f, 1 - near(f)], r1.at[it, f], s1_send.at[it, f], s1_recv.at[it, f], near_dev(f))

    def s2_copy(it, f):
        return remote(part1.at[it, f, 1 - far(f)], r2.at[it, f], s2_send.at[it, f], s2_recv.at[it, f], far_dev(f))

    def s3_copy(it, f, k):
        return remote(
            part2.at[it, f, lax.rem(hi + k, high)], r3.at[it, f, k - 1],
            s3_send.at[it, f], s3_recv.at[it, f], peers[k - 1],
        )

    def many(ref, sem):
        return pltpu.make_async_copy(ref, ref, sem)

    def g3_copy(f, k):
        own = w_next.at[f, near(f), far(f), hi]
        return remote(own, own, g3_send.at[f], g3_recv.at[f], peers[k - 1])

    def g2_copy(f, b):
        ref = w_next.at[f, near(f), b]
        return remote(ref, ref, g2_send.at[f], g2_recv.at[f], far_dev(f))

    def g1_copy(f, a):
        ref = w_next.at[f, a]
        return remote(ref, ref, g1_send.at[f], g1_recv.at[f], near_dev(f))

    for it in range(ITERS):
        power[...] = jnp.zeros_like(power)

        def make_sources(f, carry):
            if it > 0:
                g1_copy(f, 1 - near(f)).wait_recv()
            for d in range(group):
                yd, ld, hd = d % 2, d // 2 % 2, d // 4
                if it == 0:
                    block = w_in[f, hd, ld, yd]
                else:
                    block = w_next[f, yd + swapped(f) * (ld - yd), ld + swapped(f) * (yd - ld), hd]
                q = yd * (group // 2) + d // 2
                flat[f, q * rows:(q + 1) * rows, :] = block
            wr = flat[f, :, :width].astype(jnp.bfloat16)
            wi = flat[f, :, width:].astype(jnp.bfloat16)
            xr = sig[f, 0]
            xi = sig[f, 1]
            yr = dot(wr, xr) - dot(wi, xi)
            yi = dot(wr, xi) + dot(wi, xr)
            src[f, 0] = yr
            src[f, 1] = yi
            power[...] += yr * yr + yi * yi
            return carry

        lax.fori_loop(0, nb, make_sources, 0)

        def piece(parity, which):
            return pl.ds(pl.multiple_of(parity * half + which * quarter, quarter), quarter)

        def exchange(c, step, parity):
            source = power.at[piece(parity, core_o)] if step == 0 else pw_sum.at[it, c, step - 1]
            return remote(
                source, pw_recv.at[it, c, step], pw_send_sem.at[it, c, step],
                pw_recv_sem.at[it, c, step], x_dev if step == 1 else core_dev,
            )

        def add(c, step, parity):
            before = power[piece(parity, core), :] if step == 0 else pw_sum[it, c, step - 1]
            exchange(c, step, parity).wait()
            pw_sum[it, c, step] = before + pw_recv[it, c, step]
            exchange(c, step + 1, parity).start()

        def finish(c, parity):
            rinv[piece(parity, core), :] = 1.0 / jnp.sqrt(pw_sum[it, c, 1] / bins + small_eps)
            exchange(c, 2, parity).wait()
            rinv[piece(parity, core_o), :] = 1.0 / jnp.sqrt(pw_recv[it, c, 2] / bins + small_eps)

        def make_gram(parity, f):
            its_rows = pl.ds(pl.multiple_of(parity * half, half), half)
            inv = rinv[its_rows, :]
            pr = (src[f, 0, its_rows, :] * inv).astype(jnp.bfloat16)
            pi = (src[f, 1, its_rows, :] * inv).astype(jnp.bfloat16)
            br = src[f, 0].astype(jnp.bfloat16)
            bi = src[f, 1].astype(jnp.bfloat16)
            real = dot_nt(pr, br) + dot_nt(pi, bi)
            imag = dot_nt(pi, br) - dot_nt(pr, bi)
            for e in range(group // 2):
                ld, hd = e % 2, e // 2
                na, fa = parity + swapped(f) * (ld - parity), ld + swapped(f) * (parity - ld)
                gram[it, f, na, fa, hd, :, :width] = real[e * rows:(e + 1) * rows]
                gram[it, f, na, fa, hd, :, width:] = imag[e * rows:(e + 1) * rows]

        def away(f, carry):
            make_gram(1 - y, f)
            pl.when(swapped(f) == 0)(lambda: s1_copy(it, f).start())
            return carry

        def kept(f, carry):
            make_gram(y, f)
            pl.when(swapped(f) == 1)(lambda: s1_copy(it, f).start())
            return carry

        exchange(0, 0, 1 - y).start()
        add(0, 0, 1 - y)
        exchange(1, 0, y).start()
        add(0, 1, 1 - y)
        add(1, 0, y)
        finish(0, 1 - y)
        lax.fori_loop(0, nb, away, 0)
        add(1, 1, y)
        finish(1, y)
        lax.fori_loop(0, nb, kept, 0)

        def sum1(f):
            s1_copy(it, f).wait_recv()
            part1[it, f] = gram[it, f, near(f)] + r1[it, f]
            s2_copy(it, f).start()

        def sum2(f):
            s2_copy(it, f).wait_recv()
            part2[it, f] = part1[it, f, far(f)] + r2[it, f]
            for k in range(1, high):
                s3_copy(it, f, k).start()

        def update(f):
            many(r3.at[it, f], s3_recv.at[it, f]).wait()
            acc = part2[it, f, hi]
            for k in range(high - 1):
                acc = acc + r3[it, f, k]
            acc = acc * (1.0 / frames)
            w = flat[f]
            a = jnp.dot(acc[:, :width], w, precision=lax.Precision.HIGHEST, preferred_element_type=jnp.float32)
            b = jnp.dot(acc[:, width:], w, precision=lax.Precision.HIGHEST, preferred_element_type=jnp.float32)
            own = w_in[f, hi, lo, y] if it == 0 else w_next[f, near(f), far(f), hi]
            dr = own[:, :width] - (a[:, :width] - b[:, width:])
            di = own[:, width:] - (a[:, width:] + b[:, :width])
            nr = own[:, :width] + step_size * dr
            ni = own[:, width:] + step_size * di
            if it + 1 < ITERS:
                w_next[f, near(f), far(f), hi, :, :width] = nr
                w_next[f, near(f), far(f), hi, :, width:] = ni
                for k in range(1, high):
                    g3_copy(f, k).start()
            else:
                w_out[f] = own
                d_out[f, :, :width] = dr
                d_out[f, :, width:] = di

        def spread2(f):
            others = w_next.at[f, near(f), far(f), pl.ds(0, high - 1)]
            many(others, g3_recv.at[f]).wait()
            g2_copy(f, far(f)).start()

        def spread1(f):
            g2_copy(f, 1 - far(f)).wait_recv()
            g1_copy(f, near(f)).start()

        stages = [(0, sum1), (LAGS[0], sum2), (LAGS[1], update)]
        if it + 1 < ITERS:
            stages += [(LAGS[2], spread2), (LAGS[3], spread1)]

        def pipeline(s, carry):
            for lag, stage in stages:
                inside = jnp.logical_and(s >= lag, s < nb + lag)
                pl.when(inside)(functools.partial(stage, s - lag))
            return carry

        lax.fori_loop(0, nb + stages[-1][0], pipeline, 0)

    def drain(f, carry):
        for it in range(ITERS):
            s1_copy(it, f).wait_send()
            s2_copy(it, f).wait_send()
            many(r3.at[it, f], s3_send.at[it, f]).wait()
        many(w_next.at[f, near(f), far(f), pl.ds(0, high - 1)], g3_send.at[f]).wait()
        g2_copy(f, far(f)).wait_send()
        g1_copy(f, near(f)).wait_send()
        return carry

    lax.fori_loop(0, nb, drain, 0)


def on_device(signal, demix):
    group = lax.axis_size("frame")
    bin_group = lax.axis_size("bin")
    nb, _, sensors, nt = signal.shape
    total, width2 = demix.shape[1:]
    rows = total // group
    high = group // 4
    quarter = total // 4
    f32 = jnp.float32
    out = jax.ShapeDtypeStruct((nb, rows, width2), f32)
    dma = pltpu.SemaphoreType.DMA
    vmem = pl.BlockSpec(memory_space=pltpu.VMEM)
    own, direction = pl.pallas_call(
        functools.partial(kernel, group, bin_group),
        out_shape=(out, out),
        in_specs=[vmem, vmem],
        out_specs=(vmem, vmem),
        scratch_shapes=[
            pltpu.VMEM((nb, total, width2), f32),
            pltpu.VMEM((nb, 2, 2, high, rows, width2), f32),
            pltpu.VMEM((nb, 2, total, nt), f32),
            pltpu.VMEM((ITERS, nb, 2, 2, high, rows, width2), f32),
            pltpu.VMEM((ITERS, nb, 2, high, rows, width2), f32),
            pltpu.VMEM((ITERS, nb, 2, high, rows, width2), f32),
            pltpu.VMEM((ITERS, nb, high, rows, width2), f32),
            pltpu.VMEM((ITERS, nb, high, rows, width2), f32),
            pltpu.VMEM((ITERS, nb, high - 1, rows, width2), f32),
            pltpu.VMEM((total, nt), f32),
            pltpu.VMEM((ITERS, 2, 3, quarter, nt), f32),
            pltpu.VMEM((ITERS, 2, 2, quarter, nt), f32),
            pltpu.VMEM((total, nt), f32),
            dma((ITERS, 2, 3)),
            dma((ITERS, 2, 3)),
            dma((ITERS, nb)),
            dma((ITERS, nb)),
            dma((ITERS, nb)),
            dma((ITERS, nb)),
            dma((ITERS, nb)),
            dma((ITERS, nb)),
            dma((nb,)),
            dma((nb,)),
            dma((nb,)),
            dma((nb,)),
            dma((nb,)),
            dma((nb,)),
        ],
        compiler_params=pltpu.CompilerParams(
            collective_id=0, has_side_effects=True, vmem_limit_bytes=62 * 1024 * 1024
        ),
    )(signal, demix.reshape(nb, high, 2, 2, rows, width2))
    return own + step_size * direction, direction


def solution(mesh):
    placed = (P("bin", None, None, "frame"), P("bin", None, None))
    return jax.shard_map(
        on_device,
        mesh=mesh,
        in_specs=placed,
        out_specs=(P("bin", "frame", None), P("bin", "frame", None)),
        check_vma=False,
    )
```

time: 197 us -> 175 us (0.89)
  Pallas kernels: 192 us -> 171 us
  other arithmetic: 0 us -> 2.08 us
    pallas_call x1, Pallas kernels: 192 us -> 171 us  [on_device(): pl.pallas_call(functools.partial(kernel, group, bin_group), out_shape=(ou...]
    add x0 -> x1, other arithmetic: none -> 2.08 us  [on_device(): return (own + step_size * direction, direction)]
where the time goes in v2:
time: 175 us
  Pallas kernels  171 us (98%)
  other arithmetic  2.08 us (1%)
  local copies, waits for them, and re-layouts  1.87 us (1%)
    pallas_call x1, Pallas kernels, on_device(): pl.pallas_call(functools.partial(kernel, group, bin_group), out_shape=(ou...  171 us

profile of v2, /device:TPU:0, one launch (start us, length us, event | category | flops | bytes accessed | tf_op | source)
XLA Modules:
  0.0 175.2 jit_solution(18040874717486759094)
XLA Ops:
  0.6 170.6 %shard_map.41 = (f32[8,32,512]{2,1,0:T(8,128)}, f32[8,32,512]{2,1,0:T(8,128)}) custom-call(bf16[8,2,256,256]{3,2,1,0:T(8,128)(2,1)} %sig.1, f32[8,2,2,2,32,512]{5,4,3,2,1,0:T(8,128)} %bitcast.1), custom_call_target="tpu_custom_call" | custom-call | tf_op jit(solution)/shard_map/pallas_call | solution.py:272
  171.2 2.1 %multiply_add_fusion = f32[8,32,512]{2,1,0:T(8,128)} fusion(f32[8,32,512]{2,1,0:T(8,128)} %get-tuple-element.4, f32[8,32,512]{2,1,0:T(8,128)} %get-tuple-element.9), kind=kLoop, calls=%fused_computation | loop fusion | flops 262144 | bytes 1572864 | tf_op jit(solution)/shard_map/add | solution.py:310
  173.3 1.9 %copy.5 = f32[8,32,512]{2,1,0:T(8,128)} copy(f32[8,32,512]{2,1,0:T(8,128)} %get-tuple-element.9) | data formatting | bytes 1048576
